TPU v7x, 512 devices: a whole 4x4x16 slice. The times are simulated.
512 devices in a mesh: section: 8 (over z_lo), dp: 16 (over x, z_hi, core), tensor: 4 (over y).
Axes of the slice: x: 4, y: 4, z: 16 (z_hi: 2, z_lo: 8; z = z_hi * 8 + z_lo), core: 2. Of those that a mesh axis runs over, the one named last changes fastest.
Arguments:
- norm_in: bfloat16 [8, 2048, 8192], P('section', 'dp', 'tensor'), may hold values from -20 to 20
- query_grad: bfloat16 [8, 2048, 4096], P('section', 'dp', 'tensor'), may hold values from -20 to 20
- attn_out: bfloat16 [8, 2048, 4096], P('section', 'dp', 'tensor'), may hold values from -20 to 20
- handed: bfloat16 [8, 2048, 8192], P('section', 'dp', 'tensor'), may hold values from -20 to 20
- sketch_q: bfloat16 [8, 64, 4096], P('section', None, 'tensor'), may hold values from -6 to 6
- sketch_o: bfloat16 [8, 64, 8192], P('section', None, 'tensor'), may hold values from -6 to 6
Outputs:
- lora_b_q: bfloat16 [8, 64, 8192], P('section', None, 'tensor')
- lora_a_q: float32 [8, 64, 4096], P('section', None, 'tensor')
- lora_b_o: bfloat16 [8, 64, 4096], P('section', None, 'tensor')
- lora_a_o: float32 [8, 64, 8192], P('section', None, 'tensor')
All inputs are finite; a program needn't handle non-finite values.
Results may differ from a plain program's by a relative error of at most 0.03.
Values may be sent and summed in bfloat16 or wider, within the bound.
A program may use at most 64 MiB of HBM per device.

v0:
```python
import jax
import jax.numpy as jnp
from jax import lax
from jax.sharding import PartitionSpec as P

D = 8192
HQ = 4096
RANK = 64
POWER = 2
precise = lax.Precision.HIGHEST


def from_behind(value, axis, steps):
    count = lax.axis_size(axis)
    pairs = [(source, (source + steps) % count) for source in range(count)]
    return lax.ppermute(value, axis, pairs)


def gram_of(row_block):
    return jnp.dot(row_block, row_block.T, precision=precise, preferred_element_type=jnp.float32)


def solve_rows(gram_rows, row_block):
    low_factor = jnp.linalg.cholesky(gram_rows)
    solved = lax.linalg.triangular_solve(low_factor, row_block, left_side=True, lower=True)
    return solved.astype(jnp.bfloat16)


def tokens_of(sketches, matrices):
    first_part = jnp.einsum(
        "km,tm->kt", sketches[0], matrices[0], preferred_element_type=jnp.float32
    )
    second_part = jnp.einsum(
        "km,tm->kt", sketches[1], matrices[1], preferred_element_type=jnp.float32
    )
    total_a, total_b = (
        lax.psum(first_part.astype(jnp.bfloat16), "tensor").astype(jnp.float32),
        lax.psum(second_part.astype(jnp.bfloat16), "tensor").astype(jnp.float32),
    )
    return (total_a.astype(jnp.bfloat16), total_b.astype(jnp.bfloat16))


def partials(token_rows, matrices):
    part_a = jnp.dot(token_rows[0], matrices[0], preferred_element_type=jnp.float32)
    part_b = jnp.dot(token_rows[1], matrices[1], preferred_element_type=jnp.float32)
    return (part_a, part_b)


def orthonormal(partial_value):
    part_a, part_b = partial_value
    rows_a, rows_b = (
        lax.psum(part_a.astype(jnp.bfloat16), "dp").astype(jnp.float32),
        lax.psum(part_b.astype(jnp.bfloat16), "dp").astype(jnp.float32),
    )
    gram_a, gram_b = (
        lax.psum(gram_of(rows_a).astype(jnp.bfloat16), "tensor").astype(jnp.float32),
        lax.psum(gram_of(rows_b).astype(jnp.bfloat16), "tensor").astype(jnp.float32),
    )
    basis_a = solve_rows(gram_a, rows_a)
    basis_b = solve_rows(gram_b, rows_b)
    return (basis_a, basis_b)


def body(norm_in, query_grad, attn_out, handed, sketch_q, sketch_o):
    upstream = from_behind(handed, "section", -1)
    lefts = (norm_in[0], attn_out[0])
    rights = (query_grad[0], upstream[0])
    basis = orthonormal(partials(tokens_of((sketch_q[0], sketch_o[0]), rights), lefts))
    for iteration in range(POWER):
        other = orthonormal(partials(tokens_of(basis, lefts), rights))
        basis = orthonormal(partials(tokens_of(other, rights), lefts))
    final = partials(tokens_of(basis, lefts), rights)
    raw_a, raw_b = (
        lax.psum(final[0].astype(jnp.bfloat16), "dp").astype(jnp.float32),
        lax.psum(final[1].astype(jnp.bfloat16), "dp").astype(jnp.float32),
    )
    energy_a, energy_b = lax.psum((jnp.sum(raw_a * raw_a), jnp.sum(raw_b * raw_b)), "tensor")
    adapter_aq = raw_a / jnp.sqrt(energy_a / (RANK * HQ) + 1e-06)
    adapter_ao = raw_b / jnp.sqrt(energy_b / (RANK * D) + 1e-06)
    adapter_bq = basis[0] * 16.0
    adapter_bo = basis[1] * 16.0
    return (adapter_bq[None], adapter_aq[None], adapter_bo[None], adapter_ao[None])


def solution(mesh):
    return jax.shard_map(
        body,
        mesh=mesh,
        in_specs=(
            P("section", "dp", "tensor"),
            P("section", "dp", "tensor"),
            P("section", "dp", "tensor"),
            P("section", "dp", "tensor"),
            P("section", None, "tensor"),
            P("section", None, "tensor"),
        ),
        out_specs=(
            P("section", None, "tensor"),
            P("section", None, "tensor"),
            P("section", None, "tensor"),
            P("section", None, "tensor"),
        ),
        check_vma=False,
    )
```

profile of v0, /device:TPU:32, one launch (start us, length us, event | category | flops | bytes accessed | tf_op | source)
XLA Modules:
  0.0 1890.0 jit_solution(17088234802325009747)
XLA Ops:
  7.2 7.5 collective-permute-start
  16.0 7.3 collective-permute-done
  23.6 17.3 all-reduce.17
  42.9 262.2 %all-reduce.35.cloned.1.call-done = (bf16[64,2048]{1,0:T(8,128)(2,1)}, bf16[64,1024]{1,0:T(8,128)(2,1)}) async-done(((bf16[64,2048]{1,0:T(8,128)(2,1)}, bf16[64,1024]{1,0:T(8,128)(2,1)}), (bf16[64,2048]{1,0:T(8,128)(2,1)}, bf16[64,1024]{1,0:T(8,128)(2,1)})) %all-reduce.35.cloned.1.call-update) | async-done | bytes 393232 | tf_op jit(solution)/shard_map/psum | solution.py:52
  306.5 17.1 all-reduce.16
  323.8 5.8 cholesky.219
  336.6 5.8 cholesky.164
  349.6 14.5 all-reduce.15
  366.0 251.3 %all-reduce.33.cloned.1.call-done = (bf16[64,1024]{1,0:T(8,128)(2,1)}, bf16[64,2048]{1,0:T(8,128)(2,1)}) async-done(((bf16[64,1024]{1,0:T(8,128)(2,1)}, bf16[64,2048]{1,0:T(8,128)(2,1)}), (bf16[64,1024]{1,0:T(8,128)(2,1)}, bf16[64,2048]{1,0:T(8,128)(2,1)})) %all-reduce.33.cloned.1.call-update) | async-done | bytes 393232 | tf_op jit(solution)/shard_map/psum | solution.py:52
  618.7 17.1 all-reduce.14
  635.8 5.8 cholesky.230
  648.7 5.8 cholesky.175
  661.7 14.5 all-reduce.13
  678.1 251.2 %all-reduce.31.cloned.1.call-done = (bf16[64,2048]{1,0:T(8,128)(2,1)}, bf16[64,1024]{1,0:T(8,128)(2,1)}) async-done(((bf16[64,2048]{1,0:T(8,128)(2,1)}, bf16[64,1024]{1,0:T(8,128)(2,1)}), (bf16[64,2048]{1,0:T(8,128)(2,1)}, bf16[64,1024]{1,0:T(8,128)(2,1)})) %all-reduce.31.cloned.1.call-update) | async-done | bytes 393232 | tf_op jit(solution)/shard_map/psum | solution.py:52
  930.7 17.3 all-reduce.12
  948.1 5.8 cholesky.241
  955.3 4.9 custom-call.23
  961.0 5.8 cholesky.186
  974.0 14.5 all-reduce.11
  990.3 251.2 %all-reduce.29.cloned.1.call-done = (bf16[64,1024]{1,0:T(8,128)(2,1)}, bf16[64,2048]{1,0:T(8,128)(2,1)}) async-done(((bf16[64,1024]{1,0:T(8,128)(2,1)}, bf16[64,2048]{1,0:T(8,128)(2,1)}), (bf16[64,1024]{1,0:T(8,128)(2,1)}, bf16[64,2048]{1,0:T(8,128)(2,1)})) %all-reduce.29.cloned.1.call-update) | async-done | bytes 393232 | tf_op jit(solution)/shard_map/psum | solution.py:52
  1243.0 17.1 all-reduce.10
  1260.2 5.8 cholesky.252
  1267.4 4.9 custom-call.24
  1273.0 5.8 cholesky.197
  1286.1 14.5 all-reduce.9
  1302.5 251.1 %all-reduce.27.cloned.1.call-done = (bf16[64,2048]{1,0:T(8,128)(2,1)}, bf16[64,1024]{1,0:T(8,128)(2,1)}) async-done(((bf16[64,2048]{1,0:T(8,128)(2,1)}, bf16[64,1024]{1,0:T(8,128)(2,1)}), (bf16[64,2048]{1,0:T(8,128)(2,1)}, bf16[64,1024]{1,0:T(8,128)(2,1)})) %all-reduce.27.cloned.1.call-update) | async-done | bytes 393232 | tf_op jit(solution)/shard_map/psum | solution.py:52
  1555.0 17.3 all-reduce.8
  1572.4 5.8 cholesky.263
  1585.3 5.8 cholesky.208
  1598.3 14.5 all-reduce.7
  1615.3 250.7 %all-reduce.25.cloned.1.call-done = (bf16[64,1024]{1,0:T(8,128)(2,1)}, bf16[64,2048]{1,0:T(8,128)(2,1)}) async-done(((bf16[64,1024]{1,0:T(8,128)(2,1)}, bf16[64,2048]{1,0:T(8,128)(2,1)}), (bf16[64,1024]{1,0:T(8,128)(2,1)}, bf16[64,2048]{1,0:T(8,128)(2,1)})) %all-reduce.25.cloned.1.call-update) | async-done | bytes 393232 | tf_op jit(solution)/shard_map/psum | solution.py:74
  1869.1 11.1 all-reduce
  (151 shorter events, 86.0 us)
Async XLA Ops:
  7.2 33.8 %copy-start = (bf16[1,128,2048]{2,1,0:T(8,128)(2,1)S(1)}, bf16[1,128,2048]{2,1,0:T(8,128)(2,1)}, u32[]{:S(2)}) copy-start(bf16[1,128,2048]{2,1,0:T(8,128)(2,1)} %param.11) | copy-start | bytes 1572868
  7.2 16.1 copy-start.15
  7.2 297.9 %all-reduce.35.cloned.1.call-start = ((), (), s32[]{:S(2)}) async-start(), calls=%async_computation.5 | async-start | bytes 786432 | tf_op jit(solution)/shard_map/psum | solution.py:52
  7.2 16.1 collective-permute-start
  41.0 1.0 copy-start.1
  42.8 574.4 %all-reduce.33.cloned.1.call-start = ((), (), s32[]{:S(2)}) async-start(), calls=%async_computation.4 | async-start | bytes 786432 | tf_op jit(solution)/shard_map/psum | solution.py:52
  305.1 1.2 copy-start.3
  323.8 12.1 copy-start.10
  349.3 14.8 copy-start.2
  365.9 563.4 %all-reduce.31.cloned.1.call-start = ((), (), s32[]{:S(2)}) async-start(), calls=%async_computation.3 | async-start | bytes 786432 | tf_op jit(solution)/shard_map/psum | solution.py:52
  617.2 1.2 copy-start.6
  648.6 12.2 copy-start.8
  678.1 563.5 %all-reduce.29.cloned.1.call-start = ((), (), s32[]{:S(2)}) async-start(), calls=%async_computation.2 | async-start | bytes 786432 | tf_op jit(solution)/shard_map/psum | solution.py:52
  929.3 1.2 copy-start.4
  930.7 29.5 %copy-start.11 = (bf16[64,1024]{1,0:T(8,128)(2,1)S(1)}, bf16[64,1024]{1,0:T(8,128)(2,1)}, u32[]{:S(2)}) copy-start(bf16[64,1024]{1,0:T(8,128)(2,1)} %get-tuple-element.16) | copy-start | bytes 393220
  990.3 563.3 %all-reduce.27.cloned.1.call-start = ((), (), s32[]{:S(2)}) async-start(), calls=%async_computation.1 | async-start | bytes 786432 | tf_op jit(solution)/shard_map/psum | solution.py:52
  1241.6 1.2 copy-start.7
  1272.9 12.2 copy-start.9
  1302.4 563.6 %all-reduce.25.cloned.1.call-start = ((), (), s32[]{:S(2)}) async-start(), calls=%async_computation | async-start | bytes 786432 | tf_op jit(solution)/shard_map/psum | solution.py:74
  1553.6 1.2 copy-start.5
  1555.0 29.5 %copy-start.12 = (bf16[64,1024]{1,0:T(8,128)(2,1)S(1)}, bf16[64,1024]{1,0:T(8,128)(2,1)}, u32[]{:S(2)}) copy-start(bf16[64,1024]{1,0:T(8,128)(2,1)} %get-tuple-element.12) | copy-start | bytes 393220
  1866.0 1.7 copy-start.14
  1867.7 13.1 copy-start.13
Sparse Core Ops, SparseCore 0:
  42.9 262.0 all-reduce.34
  366.0 251.1 all-reduce.32
  678.2 251.0 all-reduce.30
  990.4 251.1 all-reduce.28
  1302.5 251.0 all-reduce.26
  1614.7 251.2 all-reduce.24
where the time goes:
time: 1890 us
  waiting for transfers between devices  1530 us (81%)
  blocking collectives  187 us (10%)
  other arithmetic  126 us (7%)
  matrix products  26.9 us (1%)
    psum x5, waiting for transfers between devices, orthonormal(): lax.psum(part_a.astype(jnp.bfloat16), 'dp').astype(jnp.float32)  1270 us
    psum x1, waiting for transfers between devices, body(): lax.psum(final[0].astype(jnp.bfloat16), 'dp').astype(jnp.float32)  251 us
    psum x6, blocking collectives, tokens_of(): lax.psum(first_part.astype(jnp.bfloat16), 'tensor').astype(jnp.float32)  89.9 us
    psum x5, blocking collectives, orthonormal(): lax.psum(gram_of(rows_a).astype(jnp.bfloat16), 'tensor').astype(jnp.float32)  85.8 us
    another operation x30, other arithmetic, solve_rows(): low_factor = jnp.linalg.cholesky(gram_rows)  65.2 us
    another operation x20, other arithmetic, solve_rows(): lax.linalg.triangular_solve(low_factor, row_block, left_side=True, lower=...  55.5 us
  transfers between devices with their start and end apart: 7, of which 7 were waited for; matrix products, arithmetic and copies ran while one was open for 0% of the time, Pallas kernels for 0%

commit v1 on v0

--- a/solution.py
+++ b/solution.py
@@ -71,7 +71,7 @@
         basis = orthonormal(partials(tokens_of(other, rights), lefts))
     final = partials(tokens_of(basis, lefts), rights)
     raw_a, raw_b = (
-        lax.psum(final[0].astype(jnp.bfloat16), "dp").astype(jnp.float32),
+        jnp.sum(lax.all_gather(final[0].astype(jnp.bfloat16), "dp"), axis=0).astype(jnp.float32),
         lax.psum(final[1].astype(jnp.bfloat16), "dp").astype(jnp.float32),
     )
     energy_a, energy_b = lax.psum((jnp.sum(raw_a * raw_a), jnp.sum(raw_b * raw_b)), "tensor")

time: 1890 us -> 2020 us (1.069)
  the two profiles are of different devices: /device:TPU:32 before, /device:TPU:2 now
where the time goes in v1:
time: 2020 us
  waiting for transfers between devices  1610 us (80%)
  blocking collectives  217 us (11%)
  other arithmetic  127 us (6%)
  matrix products  41.3 us (2%)
    psum x5, waiting for transfers between devices, orthonormal(): lax.psum(part_a.astype(jnp.bfloat16), 'dp').astype(jnp.float32)  1260 us
    psum x1, waiting for transfers between devices, orthonormal(): lax.psum(part_b.astype(jnp.bfloat16), 'dp').astype(jnp.float32)  242 us
    all_gather x1, waiting for transfers between devices, body(): lax.all_gather(final[0].astype(jnp.bfloat16), 'dp')  93.5 us
    psum x6, blocking collectives, tokens_of(): lax.psum(first_part.astype(jnp.bfloat16), 'tensor').astype(jnp.float32)  86.6 us
    psum x5, blocking collectives, orthonormal(): lax.psum(gram_of(rows_a).astype(jnp.bfloat16), 'tensor').astype(jnp.float32)  85.3 us
    another operation x30, other arithmetic, solve_rows(): low_factor = jnp.linalg.cholesky(gram_rows)  65.2 us
    another operation x20, other arithmetic, solve_rows(): lax.linalg.triangular_solve(low_factor, row_block, left_side=True, lower=...  55.5 us
  transfers between devices with their start and end apart: 8, of which 8 were waited for; matrix products, arithmetic and copies ran while one was open for 0% of the time, Pallas kernels for 0%

profile of v1, /device:TPU:2, one launch (start us, length us, event | category | flops | bytes accessed | tf_op | source)
XLA Modules:
  0.0 2023.7 jit_solution(875634426033747834)
XLA Ops:
  7.2 13.3 collective-permute-start
  20.5 11.5 collective-permute-done
  33.3 17.2 psum.262
  53.5 242.3 %all-reduce.22.cloned.1.call-done = bf16[64,1024]{1,0:T(8,128)(2,1)} async-done(((bf16[64,1024]{1,0:T(8,128)(2,1)}), bf16[64,1024]{1,0:T(8,128)(2,1)}) %all-reduce.22.cloned.1.call-update) | async-done | bytes 131088 | tf_op jit(solution)/shard_map/psum | solution.py:53
  297.0 16.9 psum.264
  314.0 5.8 cholesky.219
  327.7 14.5 all-reduce.14
  344.1 252.9 %all-reduce.32.cloned.1.call-done = (bf16[64,2048]{1,0:T(8,128)(2,1)}, bf16[64,2048]{1,0:T(8,128)(2,1)}) async-done(((bf16[64,2048]{1,0:T(8,128)(2,1)}, bf16[64,2048]{1,0:T(8,128)(2,1)}), (bf16[64,2048]{1,0:T(8,128)(2,1)}, bf16[64,2048]{1,0:T(8,128)(2,1)})) %all-reduce.32.cloned.1.call-update) | async-done | bytes 524304 | tf_op jit(solution)/shard_map/psum | solution.py:52
  599.6 17.1 all-reduce.13
  616.9 5.8 cholesky.230
  643.9 14.5 all-reduce.12
  660.1 250.6 %all-reduce.30.cloned.1.call-done = (bf16[64,1024]{1,0:T(8,128)(2,1)}, bf16[64,1024]{1,0:T(8,128)(2,1)}) async-done(((bf16[64,1024]{1,0:T(8,128)(2,1)}, bf16[64,1024]{1,0:T(8,128)(2,1)}), (bf16[64,1024]{1,0:T(8,128)(2,1)}, bf16[64,1024]{1,0:T(8,128)(2,1)})) %all-reduce.30.cloned.1.call-update) | async-done | bytes 262160 | tf_op jit(solution)/shard_map/psum | solution.py:52
  913.1 17.1 all-reduce.11
  930.3 5.8 cholesky.241
  944.0 5.8 cholesky.175
  957.6 14.5 all-reduce.10
  974.0 253.1 %all-reduce.28.cloned.1.call-done = (bf16[64,2048]{1,0:T(8,128)(2,1)}, bf16[64,2048]{1,0:T(8,128)(2,1)}) async-done(((bf16[64,2048]{1,0:T(8,128)(2,1)}, bf16[64,2048]{1,0:T(8,128)(2,1)}), (bf16[64,2048]{1,0:T(8,128)(2,1)}, bf16[64,2048]{1,0:T(8,128)(2,1)})) %all-reduce.28.cloned.1.call-update) | async-done | bytes 524304 | tf_op jit(solution)/shard_map/psum | solution.py:52
  1229.7 17.1 all-reduce.9
  1246.9 5.8 cholesky.252
  1260.7 5.8 cholesky.186
  1274.0 14.5 all-reduce.8
  1290.2 250.6 %all-reduce.26.cloned.1.call-done = (bf16[64,1024]{1,0:T(8,128)(2,1)}, bf16[64,1024]{1,0:T(8,128)(2,1)}) async-done(((bf16[64,1024]{1,0:T(8,128)(2,1)}, bf16[64,1024]{1,0:T(8,128)(2,1)}), (bf16[64,1024]{1,0:T(8,128)(2,1)}, bf16[64,1024]{1,0:T(8,128)(2,1)})) %all-reduce.26.cloned.1.call-update) | async-done | bytes 262160 | tf_op jit(solution)/shard_map/psum | solution.py:52
  1543.2 17.1 all-reduce.7
  1560.4 5.8 cholesky.263
  1574.1 5.8 cholesky.197
  1587.7 14.5 all-reduce.6
  1604.1 253.0 %all-reduce.24.cloned.1.call-done = (bf16[64,2048]{1,0:T(8,128)(2,1)}, bf16[64,2048]{1,0:T(8,128)(2,1)}) async-done(((bf16[64,2048]{1,0:T(8,128)(2,1)}, bf16[64,2048]{1,0:T(8,128)(2,1)}), (bf16[64,2048]{1,0:T(8,128)(2,1)}, bf16[64,2048]{1,0:T(8,128)(2,1)})) %all-reduce.24.cloned.1.call-update) | async-done | bytes 524304 | tf_op jit(solution)/shard_map/psum | solution.py:52
  1858.4 16.9 psum.259
  1875.4 5.8 cholesky.208
  1889.4 14.3 psum.260
  1906.0 93.5 %all-gather.3.cloned.1.call-done = bf16[1024,1024]{1,0:T(8,128)(2,1)} async-done(((bf16[64,1024]{1,0:T(8,128)(2,1)}), bf16[1024,1024]{1,0:T(8,128)(2,1)}) %all-gather.3.cloned.1.call-update) | async-done | bytes 2097168 | tf_op jit(solution)/shard_map/all_gather | solution.py:74
  2002.8 11.1 all-reduce
  (137 shorter events, 117.1 us)
Async XLA Ops:
  7.2 335.0 %copy-start = (bf16[1,128,2048]{2,1,0:T(8,128)(2,1)S(1)}, bf16[1,128,2048]{2,1,0:T(8,128)(2,1)}, u32[]{:S(2)}) copy-start(bf16[1,128,2048]{2,1,0:T(8,128)(2,1)} %param.11) | copy-start | bytes 1572868
  7.2 320.3 %copy-start.1 = (bf16[1,128,1024]{2,1,0:T(8,128)(2,1)S(1)}, bf16[1,128,1024]{2,1,0:T(8,128)(2,1)}, u32[]{:S(2)}) copy-start(bf16[1,128,1024]{2,1,0:T(8,128)(2,1)} %param.13) | copy-start | bytes 786436
  7.2 288.7 %all-reduce.22.cloned.1.call-start = ((), (), s32[]{:S(2)}) async-start(), calls=%async_computation | async-start | bytes 262144 | tf_op jit(solution)/shard_map/psum | solution.py:53
  7.2 24.8 %collective-permute-start = (bf16[1,128,2048]{2,1,0:T(8,128)(2,1)}, bf16[1,128,2048]{2,1,0:T(8,128)(2,1)S(1)}, u32[]{:S(2)}, u32[]{:S(2)}) collective-permute-start(bf16[1,128,2048]{2,1,0:T(8,128)(2,1)} %param.14), channel_id=1, source_target_pairs={{0,448},{64,0},{128,64},{192,128},{256,192},{320,256},{384,320},{4... | collective-permute-start | bytes 1572872 | tf_op jit(solution)/shard_map/ppermute | solution.py:16
  52.2 544.8 %all-reduce.32.cloned.1.call-start = ((), (), s32[]{:S(2)}) async-start(), calls=%async_computation.6 | async-start | bytes 1048576 | tf_op jit(solution)/shard_map/psum | solution.py:52
  344.0 566.8 %all-reduce.30.cloned.1.call-start = ((), (), s32[]{:S(2)}) async-start(), calls=%async_computation.5 | async-start | bytes 524288 | tf_op jit(solution)/shard_map/psum | solution.py:52
  597.0 45.7 %copy-start.3 = (bf16[64,2048]{1,0:T(8,128)(2,1)S(1)}, bf16[64,2048]{1,0:T(8,128)(2,1)}, u32[]{:S(2)}) copy-start(bf16[64,2048]{1,0:T(8,128)(2,1)} %get-tuple-element.17) | copy-start | bytes 786436
  598.3 60.9 %copy-start.2 = (bf16[1,128,1024]{2,1,0:T(8,128)(2,1)S(1)}, bf16[1,128,1024]{2,1,0:T(8,128)(2,1)}, u32[]{:S(2)}) copy-start(bf16[1,128,1024]{2,1,0:T(8,128)(2,1)} %param.12) | copy-start | bytes 786436
  660.1 567.1 %all-reduce.28.cloned.1.call-start = ((), (), s32[]{:S(2)}) async-start(), calls=%async_computation.4 | async-start | bytes 1048576 | tf_op jit(solution)/shard_map/psum | solution.py:52
  974.0 566.9 %all-reduce.26.cloned.1.call-start = ((), (), s32[]{:S(2)}) async-start(), calls=%async_computation.3 | async-start | bytes 524288 | tf_op jit(solution)/shard_map/psum | solution.py:52
  1227.1 45.6 %copy-start.4 = (bf16[64,2048]{1,0:T(8,128)(2,1)S(1)}, bf16[64,2048]{1,0:T(8,128)(2,1)}, u32[]{:S(2)}) copy-start(bf16[64,2048]{1,0:T(8,128)(2,1)} %get-tuple-element.13) | copy-start | bytes 786436
  1290.2 567.0 %all-reduce.24.cloned.1.call-start = ((), (), s32[]{:S(2)}) async-start(), calls=%async_computation.2 | async-start | bytes 1048576 | tf_op jit(solution)/shard_map/psum | solution.py:52
  1604.1 395.4 %all-gather.3.cloned.1.call-start = ((), (), s32[]{:S(2)}) async-start(), calls=%async_computation.1 | async-start | bytes 2228224 | tf_op jit(solution)/shard_map/all_gather | solution.py:74
  1857.1 48.1 %copy-start.5 = (bf16[64,2048]{1,0:T(8,128)(2,1)S(1)}, bf16[64,2048]{1,0:T(8,128)(2,1)}, u32[]{:S(2)}) copy-start(bf16[64,2048]{1,0:T(8,128)(2,1)} %get-tuple-element.10) | copy-start | bytes 786436
Sparse Core Ops, SparseCore 0:
  52.4 243.4 all-reduce.21
  344.1 252.8 all-reduce.31
  660.2 250.5 all-reduce.29
  974.1 252.9 all-reduce.27
  1290.3 250.5 all-reduce.25
  1604.2 252.8 all-reduce.23
  1904.7 94.7 all-gather.2
